TPU v7x, 256 devices: a whole 4x4x8 slice. The times are simulated.
256 devices in a mesh: prefix: 8 (over x, core), sample: 32 (over y, z).
Axes of the slice: x: 4, y: 4, z: 8, core: 2. Of those that a mesh axis runs over, the one named last changes fastest.
Arguments:
- hidden_states: bfloat16 [128, 8192], P(None, 'sample'), may hold values from -400 to 400
- query_weight: bfloat16 [8192, 8192], P('sample', 'prefix'), may hold values from -0.044194174 to 0.044194174
- prefix_levels: bfloat16 [2, 4096, 8, 128], P(None, 'prefix'), may hold values from -127 to 127, as said below
- prefix_scale: float32 [2, 32, 8], P(None, 'prefix'), may hold values from 0.004 to 1
- suffix_cache: bfloat16 [2, 128, 4096, 8, 128], P(None, 'sample', 'prefix'), may hold values from -12 to 12
- lengths: int32 [128], P('sample'), may hold values from 1 to 4096, 262144 in all
- output_weight: bfloat16 [8192, 8192], P('prefix', 'sample'), may hold values from -0.0625 to 0.0625
Outputs:
- mixed: bfloat16 [128, 8192], P('prefix', 'sample')
Inputs may be any that keep to these rules, and one draw needn't show every extreme that they name: Sample b's suffix cache is live at positions below lengths[b]; some sample has exactly 4096. `prefix_levels`: whole numbers.
All inputs are finite; a program needn't handle non-finite values. No bound on the sum of `lengths` on one device may be relied on, other than what follows from the above.
Results may differ from a plain program's by a relative error of at most 0.02.
Values may be sent and summed in bfloat16 or wider, within the bound.
A program may use at most 64 MiB of HBM per device.

v0:
```python
import math

import jax
import jax.numpy as jnp
from jax import lax
from jax.sharding import Mesh
from jax.sharding import PartitionSpec as P

D = 8192
BLOCK = 128
PREFIX = ("prefix_0", "prefix_1")


epsilon = 1e-05


def split_up(x, dim, size):
    shape = x.shape
    parts = x.reshape(*shape[:dim], size, shape[dim] // size, *shape[dim + 1 :])
    return jnp.moveaxis(parts, dim, 0)


def summed_on_arrival(x, axis, dim):
    size = lax.axis_size(axis)
    parts = lax.all_to_all(split_up(x, dim, size), axis, 0, 0, tiled=True)
    return jnp.sum(parts, axis=0)


def in_one_piece(arrays, axis, dim, along):
    columns = [a.reshape(*a.shape[:along], -1) for a in arrays]
    both = jnp.concatenate(columns, axis=along)
    out, at, outs = (summed_on_arrival(both, axis, dim), 0, [])
    for a, column in zip(arrays, columns):
        share = out[..., at : at + column.shape[along]]
        outs.append(share.reshape(*share.shape[:along], *a.shape[along:]))
        at += column.shape[along]
    return tuple(outs)


def copy_for_each(x, axis):
    copies = jnp.broadcast_to(x, (lax.axis_size(axis), *x.shape))
    return lax.all_to_all(copies, axis, split_axis=0, concat_axis=0, tiled=True)


def laid_out(parts, dim):
    shape = list(parts.shape[1:])
    shape[dim] *= parts.shape[0]
    return jnp.moveaxis(parts, 0, dim).reshape(shape)


def gathered_copies(x, axis, dim):
    parts = copy_for_each(x, axis)
    return laid_out(parts, dim)


def all_in_one(x, axis):
    leaves = jax.tree.leaves(x)
    sequence = sorted(range(len(leaves)), key=lambda k: -leaves[k].size)
    width = (1, *leaves[sequence[0]].shape)[-1]
    lines = [
        jnp.pad(leaves[k].reshape(-1), (0, -leaves[k].size % width)).reshape(-1, width)
        for k in sequence
    ]
    both, at, found = (lax.all_gather(jnp.concatenate(lines), axis), 0, {})
    for k, line in zip(sequence, lines):
        share = both[:, at : at + len(line)].reshape(len(both), -1)
        found[k] = share[:, : leaves[k].size].reshape(-1, *leaves[k].shape)
        at += len(line)
    numbers = iter(range(len(leaves)))
    return jax.tree.map(lambda _: found[next(numbers)], x)


def combined_by_axis(x, axes, combine):
    for axis in axes:
        pieces = all_in_one(x, axis)
        x = jax.tree.map(lambda part: part[0], pieces)
        for k in range(1, lax.axis_size(axis)):
            x = combine(x, jax.tree.map(lambda part: part[k], pieces))
    return x


def summed_on_arrival_2(x, axis, dim):
    size = lax.axis_size(axis)
    parts = lax.all_to_all(split_up(x, dim, size), axis, 0, 0, tiled=True)
    return jnp.sum(parts.astype(jnp.float32), axis=0)


def combine_parts(earlier, second):
    peak_one, total_one, values_one = earlier
    peak_two, total_two, values_two = second
    top_score = jnp.maximum(peak_one, peak_two)
    factor_one = jnp.exp(peak_one - top_score)
    factor_two = jnp.exp(peak_two - top_score)
    return (
        top_score,
        total_one * factor_one + total_two * factor_two,
        values_one * factor_one[..., None] + values_two * factor_two[..., None],
    )


def on_device(
    hidden_states, query_weight, prefix_levels, prefix_scale, suffix_cache, lengths, output_weight
):
    own_rows = lengths.shape[0]
    squares = jnp.sum(jnp.square(hidden_states.astype(jnp.float32)), axis=1)
    partial_value = jnp.dot(hidden_states, query_weight, preferred_element_type=jnp.float32)
    summed, own_squares = in_one_piece((partial_value, squares), "sample", 0, 1)
    queries = (summed * lax.rsqrt(own_squares / D + epsilon)[:, None]).astype(jnp.bfloat16)
    heads_all = gathered_copies(queries, PREFIX, 1)
    groups = prefix_levels.shape[2]
    head_size = prefix_levels.shape[3]
    heads_total = heads_all.shape[1] // head_size
    per_group = heads_total // groups
    grouped = heads_all.reshape(own_rows, groups, per_group, head_size)
    scaling = 1.0 / math.sqrt(head_size)
    tokens = prefix_levels.shape[1]
    blocks = prefix_scale.shape[1]
    raw_scores = jnp.einsum(
        "bgrd,tgd->gbrt", grouped, prefix_levels[0], preferred_element_type=jnp.float32
    )
    key_scale = jnp.transpose(prefix_scale[0])[:, None, None, :, None]
    prefix_scores = (
        raw_scores.reshape(groups, own_rows, per_group, blocks, BLOCK) * key_scale * scaling
    )
    suffix_span = suffix_cache.shape[2]
    suffix_raw = (
        jnp.einsum("bgrd,btgd->gbrt", grouped, suffix_cache[0], preferred_element_type=jnp.float32)
        * scaling
    )
    positions = lax.axis_index(PREFIX) * suffix_span + jnp.arange(suffix_span, dtype=jnp.int32)
    live_mask = positions[None, :] < lengths[:, None]
    suffix_scores = jnp.where(live_mask[None, :, None, :], suffix_raw, -jnp.inf)
    top_score = jnp.maximum(jnp.max(prefix_scores, axis=(3, 4)), jnp.max(suffix_scores, axis=3))
    prefix_exp = jnp.exp(prefix_scores - top_score[..., None, None])
    suffix_exp = jnp.exp(suffix_scores - top_score[..., None])
    denominator = jnp.sum(prefix_exp, axis=(3, 4)) + jnp.sum(suffix_exp, axis=3)
    value_scale = jnp.transpose(prefix_scale[1])[:, None, None, :, None]
    prefix_weights = (
        (prefix_exp * value_scale).reshape(groups, own_rows, per_group, tokens).astype(jnp.bfloat16)
    )
    suffix_weights = suffix_exp.astype(jnp.bfloat16)
    weighted = jnp.einsum(
        "gbrt,tgd->gbrd", prefix_weights, prefix_levels[1], preferred_element_type=jnp.float32
    )
    weighted = weighted + jnp.einsum(
        "gbrt,btgd->gbrd", suffix_weights, suffix_cache[1], preferred_element_type=jnp.float32
    )
    peak_heads = jnp.transpose(top_score, (1, 0, 2)).reshape(own_rows, heads_total)
    total_heads = jnp.transpose(denominator, (1, 0, 2)).reshape(own_rows, heads_total)
    value_heads = jnp.transpose(weighted, (1, 0, 2, 3)).reshape(own_rows, heads_total, head_size)
    local_heads = heads_total // lax.axis_size(PREFIX)
    peak_all, total_all, values_all = combined_by_axis(
        (peak_heads, total_heads, value_heads), PREFIX, combine_parts
    )
    first_head = lax.axis_index(PREFIX) * local_heads
    own_total = lax.dynamic_slice_in_dim(total_all, first_head, local_heads, 1)
    own_values = lax.dynamic_slice_in_dim(values_all, first_head, local_heads, 1)
    attended = (
        (own_values / own_total[..., None])
        .reshape(own_rows, local_heads * head_size)
        .astype(jnp.bfloat16)
    )
    partial_out = jnp.dot(
        gathered_copies(attended, "sample", 0), output_weight, preferred_element_type=jnp.float32
    )
    return summed_on_arrival_2(partial_out.astype(jnp.bfloat16), PREFIX, 0).astype(jnp.bfloat16)


def solution(mesh):
    split = Mesh(
        mesh.devices.reshape(4, 2, mesh.shape["sample"]), ("prefix_0", "prefix_1", "sample")
    )
    return jax.shard_map(
        on_device,
        mesh=split,
        in_specs=(
            P(None, "sample"),
            P("sample", PREFIX),
            P(None, PREFIX, None, None),
            P(None, PREFIX, None),
            P(None, "sample", PREFIX, None, None),
            P("sample"),
            P(PREFIX, "sample"),
        ),
        out_specs=P(PREFIX, "sample"),
        check_vma=False,
    )
```

profile of v0, /device:TPU:1, one launch (start us, length us, event | category | flops | bytes accessed | tf_op | source)
XLA Modules:
  0.0 97.3 jit_solution(13084249416297184159)
XLA Ops:
  0.0 1.0 %multiply_reduce_fusion = f32[128]{0:T(128)S(1)} fusion(bf16[128,256]{1,0:T(8,128)(2,1)} %param.7), kind=kLoop, calls=%fused_computation.39 | loop fusion | flops 98176 | bytes 66048 | tf_op jit(solution)/shard_map/reduce_sum | solution.py:105
  1.1 1.1 %fusion.62 = f32[128,1024]{1,0:T(8,128)S(1)} fusion(bf16[128,256]{1,0:T(8,128)(2,1)} %param.7, bf16[256,1024]{1,0:T(8,128)(2,1)S(1)} %copy-done), kind=kOutput, calls=%fused_computation.113 | convolution fusion | flops 67108864 | bytes 1114112 | tf_op jit(solution)/shard_map/dot_general | solution.py:106
  2.1 0.1 concatenate.14
  2.3 0.2 concatenate.19
  2.6 1.0 pad_maximum_fusion
  3.5 12.0 %all-to-all-start = ((f32[32,4,1025]{2,1,0:T(4,128)}), f32[32,4,1025]{2,1,0:T(4,128)S(1)}, u32[]{:S(2)}, u32[]{:S(2)}) async-start(f32[32,4,1025]{2,1,0:T(4,128)} %pad_maximum_fusion), calls=%async_computation | async-start | bytes 1179648 | tf_op jit(solution)/shard_map/all_to_all | solution.py:25
  15.7 2.7 %fusion.57 = (bf16[1,512,8,128]{3,2,1,0:T(8,128)(2,1)S(1)}, bf16[1,512,8,128]{3,2,1,0:T(8,128)(2,1)}) fusion(bf16[2,512,8,128]{3,2,1,0:T(8,128)(2,1)} %param.9), kind=kLoop, calls=%fused_computation.108 | loop fusion | bytes 4194304 | tf_op jit(solution)/shard_map/slice | solution.py:143
  18.5 5.7 %fusion.56 = (bf16[1,4,512,8,128]{4,3,2,1,0:T(8,128)(2,1)}, bf16[1,4,512,8,128]{4,3,2,1,0:T(8,128)(2,1)}) fusion(bf16[2,4,512,8,128]{4,3,2,1,0:T(8,128)(2,1)} %param.11), kind=kLoop, calls=%fused_computation.107 | loop fusion | bytes 16777216 | tf_op jit(solution)/shard_map/slice | solution.py:146
  24.2 6.7 %all-to-all-done = f32[32,4,1025]{2,1,0:T(4,128)S(1)} async-done(((f32[32,4,1025]{2,1,0:T(4,128)}), f32[32,4,1025]{2,1,0:T(4,128)S(1)}, u32[]{:S(2)}, u32[]{:S(2)}) %all-to-all-start) | async-done | bytes 524832 | tf_op jit(solution)/shard_map/all_to_all | solution.py:25
  30.9 0.1 reduce_sum.49
  31.0 0.1 fusion.33
  31.2 0.6 broadcast_in_dim.16
  31.9 7.8 %all-to-all-start.1 = ((bf16[8,4,1024]{2,1,0:T(4,128)(2,1)}), bf16[8,4,1024]{2,1,0:T(4,128)(2,1)S(1)}, u32[]{:S(2)}, u32[]{:S(2)}) async-start(bf16[8,4,1024]{2,1,0:T(4,128)(2,1)} %broadcast_in_dim.16), calls=%async_computation.1 | async-start | bytes 131072 | tf_op jit(solution)/shard_map/all_to_all | solution.py:42
  39.7 4.8 %all-to-all-done.1 = bf16[8,4,1024]{2,1,0:T(4,128)(2,1)S(1)} async-done(((bf16[8,4,1024]{2,1,0:T(4,128)(2,1)}), bf16[8,4,1024]{2,1,0:T(4,128)(2,1)S(1)}, u32[]{:S(2)}, u32[]{:S(2)}) %all-to-all-start.1) | async-done | bytes 65568 | tf_op jit(solution)/shard_map/all_to_all | solution.py:42
  44.6 3.6 %fusion.61 = (f32[8,4,8]{2,1,0:T(4,128)S(1)}, f32[8,4,8,512]{3,2,1,0:T(8,128)S(1)}) fusion(bf16[4,8,8,128]{3,2,0,1:T(8,128)(2,1)S(1)} %reshape_reshape.2, bf16[1,4,512,8,128]{4,3,2,1,0:T(8,128)(2,1)} %get-tuple-element.15, pred[4,512]{1,0:T(4,128)(4,1)S(1)} %broadcast_compare_fusion), kind=kOutput, calls=%fused_computation.112 | convolution fusion | flops 33947392 | bytes 4787200 | tf_op jit(solution)/shard_map/bgrd,btgd->gbrt/dot_general | solution.py:127
  48.1 0.6 fusion.60
  48.7 0.3 fusion.9
  49.0 0.1 reshape.260
  49.1 0.4 fusion.7
  49.5 3.5 %fusion.6 = f32[4,8,8,128]{3,2,0,1:T(8,128)S(1)} fusion(f32[8,4,8,128]{3,2,1,0:T(8,128)S(1)} %fusion.7, bf16[1,4,512,8,128]{4,3,2,1,0:T(8,128)(2,1)} %get-tuple-element.14, f32[8,4,8,512]{3,2,1,0:T(8,128)S(1)} %get-tuple-element.34, f32[8,4,8]{2,1,0:T(4,128)S(1)} %max.85), kind=kOutput, calls=%fused_computation.9 | convolution fusion | flops 33849344 | bytes 4981760 | tf_op jit(solution)/shard_map/gbrt,btgd->gbrd/dot_general | solution.py:145
  53.0 0.1 reshape.259
  53.1 9.9 %all-gather.2 = f32[4,260,128]{2,1,0:T(8,128)S(1)} all-gather(f32[1,260,128]{2,1,0:T(8,128)S(1)} %maximum_bitcast_fusion), channel_id=2, replica_groups=mesh['prefix_0'=4,'prefix_1'=2,'sample'=32] {'prefix_0'}, dimensions={0}, use_global_device_ids=true | all-gather | bytes 665600 | tf_op jit(solution)/shard_map/all_gather | solution.py:64
  63.1 0.3 fusion.16
  63.4 6.0 %all-gather.3 = f32[2,260,128]{2,1,0:T(8,128)S(1)} all-gather(f32[1,260,128]{2,1,0:T(8,128)S(1)} %maximum_bitcast_fusion.1), channel_id=3, replica_groups=mesh['prefix_0'=4,'prefix_1'=2,'sample'=32] {'prefix_1'}, dimensions={0}, use_global_device_ids=true | all-gather | bytes 399360 | tf_op jit(solution)/shard_map/all_gather | solution.py:64
  69.4 0.1 squeeze.103
  69.5 0.1 squeeze.104
  69.6 0.1 squeeze.106
  69.9 0.1 fusion.28
  70.1 15.2 %all_to_all.20 = bf16[32,4,1024]{2,1,0:T(4,128)(2,1)S(1)} all-to-all(bf16[32,4,1024]{2,1,0:T(4,128)(2,1)S(1)} %broadcast_in_dim.19), channel_id=1, replica_groups=mesh['prefix_0'=4,'prefix_1'=2,'sample'=32] {'sample'}, dimensions={0} | all-to-all | bytes 524288 | tf_op jit(solution)/shard_map/all_to_all | solution.py:42
  85.3 0.2 convolution_convert_fusion
  85.6 11.1 %all_to_all.21 = bf16[8,16,256]{2,1,0:T(8,128)(2,1)S(1)} all-to-all(bf16[8,16,256]{2,1,0:T(8,128)(2,1)S(1)} %bitcast.214), channel_id=1, replica_groups=mesh['prefix_0'=4,'prefix_1'=2,'sample'=32] {'prefix_0','prefix_1'}, dimensions={0} | all-to-all | bytes 131072 | tf_op jit(solution)/shard_map/all_to_all | solution.py:84
  96.7 0.6 reduce_sum.52
  (36 shorter events, 0.9 us)
Async XLA Ops:
  0.0 1.1 %copy-start = (bf16[256,1024]{1,0:T(8,128)(2,1)S(1)}, bf16[256,1024]{1,0:T(8,128)(2,1)}, u32[]{:S(2)}) copy-start(bf16[256,1024]{1,0:T(8,128)(2,1)} %param.8) | copy-start | bytes 1572868
  0.0 15.6 %copy-start.3 = (f32[2,4,8]{2,1,0:T(4,128)S(1)}, f32[2,4,8]{2,1,0:T(4,128)}, u32[]{:S(2)}) copy-start(f32[2,4,8]{2,1,0:T(4,128)} %param.10) | copy-start | bytes 772
  3.5 27.4 %all-to-all-start = ((f32[32,4,1025]{2,1,0:T(4,128)}), f32[32,4,1025]{2,1,0:T(4,128)S(1)}, u32[]{:S(2)}, u32[]{:S(2)}) async-start(f32[32,4,1025]{2,1,0:T(4,128)} %pad_maximum_fusion), calls=%async_computation | async-start | bytes 1179648 | tf_op jit(solution)/shard_map/all_to_all | solution.py:25
  18.5 21.2 %copy-start.4 = (s32[4]{0:T(128)S(1)}, s32[4]{0:T(128)}, u32[]{:S(2)}) copy-start(s32[4]{0:T(128)} %param.12) | copy-start | bytes 52
  31.9 12.6 %all-to-all-start.1 = ((bf16[8,4,1024]{2,1,0:T(4,128)(2,1)}), bf16[8,4,1024]{2,1,0:T(4,128)(2,1)S(1)}, u32[]{:S(2)}, u32[]{:S(2)}) async-start(bf16[8,4,1024]{2,1,0:T(4,128)(2,1)} %broadcast_in_dim.16), calls=%async_computation.1 | async-start | bytes 131072 | tf_op jit(solution)/shard_map/all_to_all | solution.py:42
  44.6 3.6 %copy-start.1 = (bf16[1,512,8,128]{3,2,1,0:T(8,128)(2,1)S(1)}, bf16[1,512,8,128]{3,2,1,0:T(8,128)(2,1)}, u32[]{:S(2)}) copy-start(bf16[1,512,8,128]{3,2,1,0:T(8,128)(2,1)} %get-tuple-element.17) | copy-start | bytes 3145732
  49.5 35.8 %copy-start.2 = (bf16[1024,256]{1,0:T(8,128)(2,1)S(1)}, bf16[1024,256]{1,0:T(8,128)(2,1)}, u32[]{:S(2)}) copy-start(bf16[1024,256]{1,0:T(8,128)(2,1)} %param.13) | copy-start | bytes 1572868
where the time goes:
time: 97.7 us; the launch traced here: 97.3 us
  blocking collectives  42.2 us (43%)
  starting transfers between devices  19.8 us (20%)
  waiting for transfers between devices  11.5 us (12%)
  local copies, waits for them, and re-layouts  10.6 us (11%)
  matrix products  9.27 us (9%)
  other arithmetic  3.71 us (4%)
    all_gather x2, blocking collectives, all_in_one(): both, at, found = (lax.all_gather(jnp.concatenate(lines), axis), 0, {})  15.9 us
    all_to_all x1, blocking collectives, copy_for_each(): return lax.all_to_all(copies, axis, split_axis=0, concat_axis=0, tiled=True)  15.2 us
    all_to_all x1, starting transfers between devices, summed_on_arrival(): parts = lax.all_to_all(split_up(x, dim, size), axis, 0, 0, tiled=True)  12 us
    all_to_all x1, blocking collectives, summed_on_arrival_2(): parts = lax.all_to_all(split_up(x, dim, size), axis, 0, 0, tiled=True)  11.1 us
    all_to_all x1, starting transfers between devices, copy_for_each(): return lax.all_to_all(copies, axis, split_axis=0, concat_axis=0, tiled=True)  7.79 us
    all_to_all x1, waiting for transfers between devices, summed_on_arrival(): parts = lax.all_to_all(split_up(x, dim, size), axis, 0, 0, tiled=True)  6.72 us
    slice x1, local copies, waits for them, and re-layouts, on_device(): suffix_cache[1]  5.73 us
    all_to_all x1, waiting for transfers between devices, copy_for_each(): return lax.all_to_all(copies, axis, split_axis=0, concat_axis=0, tiled=True)  4.77 us
  transfers between devices with their start and end apart: 2, of which 2 were waited for; matrix products, arithmetic and copies ran while one was open for 9% of the time, Pallas kernels for 0%

commit v1 on v0

v1 whole, which is shorter than its diff:
```python
import functools
import math

import jax
import jax.numpy as jnp
from jax import lax
from jax.experimental import pallas as pl
from jax.experimental.pallas import tpu as pltpu
from jax.sharding import PartitionSpec as P

MESH = pl.DeviceIdType.MESH
EPSILON = 1e-05
BLOCK = 128
NX, NC, NY, NZ = 4, 2, 4, 8
NP = NX * NC
OWN = 4
HD = 128
GROUPS = 8
REP = 8
ROWS = OWN * REP
COLS = REP * HD
WIDE = COLS + 128
SPAN = 512
D = 8192
SCALING = 1.0 / math.sqrt(HD)
X_ORDER = (0, 1, 3, 2)
FAR_FIRST = (4, 3, 5, 2, 6, 1, 7, 0)
NEAR_FIRST = FAR_FIRST[::-1]
F32 = jnp.float32
BF16 = jnp.bfloat16


def split_lanes(values):
    folded = values + pltpu.roll(values, 64, 1)
    high = folded.astype(BF16).astype(F32)
    lane = lax.broadcasted_iota(jnp.int32, folded.shape, 1)
    return jnp.where(lane < 64, high, folded - high)


def regroup(source, target):
    tokens = 64

    @pl.loop(0, SPAN // tokens)
    def _(step):
        rows = source[pl.ds(pl.multiple_of(step * tokens * GROUPS, tokens * GROUPS), tokens * GROUPS), :]
        rows = jnp.swapaxes(rows.reshape(tokens, GROUPS, HD), 0, 1)
        target[:, pl.ds(pl.multiple_of(step * tokens, tokens), tokens), :] = rows


def across(a, b):
    return lax.dot_general(a, b, (((1,), (1,)), ((), ())), preferred_element_type=F32)


def kernel(
    scale, lengths, hidden_hbm, wq_hbm, prefix_hbm, suffix_hbm, wo_hbm, out,
    hidden, wq, wo, praw, sraw, pre, suf, partial, ysend, yrecv, mine, zsend, zrecv, qrows, qall,
    csend, crecv, heads, osend, orecv,
    load_sem, raw_sem, ys, yr, zs, zr, qs, qr, cs, cr, gs, gr, hs, hr, os_, or_,
):
    p = lax.axis_index("prefix")
    s = lax.axis_index("sample")
    x, c = p // NC, p % NC
    y, z = s // NZ, s % NZ

    def at_y(k):
        return (p, lax.rem(y + k, NY) * NZ + z)

    def at_z(k):
        return (p, y * NZ + lax.rem(z + k, NZ))

    def prefix_of(dx, dc):
        return lax.rem(x + dx, NX) * NC + lax.rem(c + dc, NC)

    def remote(src, dst, ssem, rsem, device):
        return pltpu.make_async_remote_copy(
            src_ref=src, dst_ref=dst, send_sem=ssem, recv_sem=rsem, device_id=device, device_id_type=MESH
        )

    pending = []

    def start(copy):
        copy.start()
        pending.append(copy)
        return copy

    others = [(dx, dc) for dx in X_ORDER for dc in range(NC) if dx or dc]

    load_hidden = pltpu.make_async_copy(hidden_hbm, hidden, load_sem.at[0])
    load_wq = pltpu.make_async_copy(wq_hbm, wq, load_sem.at[1])
    load_wo = pltpu.make_async_copy(wo_hbm, wo, load_sem.at[2])
    load_hidden.start()
    load_wq.start()

    barrier = pltpu.get_barrier_semaphore()
    for k in range(1, NZ):
        pl.semaphore_signal(barrier, inc=1, device_id=at_z(k), device_id_type=MESH)
    for k in range(1, NY):
        pl.semaphore_signal(barrier, inc=1, device_id=at_y(k), device_id_type=MESH)
    for dx, dc in others:
        pl.semaphore_signal(barrier, inc=1, device_id=(prefix_of(dx, dc), s), device_id_type=MESH)

    load_hidden.wait()
    load_wq.wait()

    raw = []
    for side in range(2):
        for i in range(OWN):
            raw.append(
                (
                    pltpu.make_async_copy(suffix_hbm.at[side, i], sraw.at[side, i], raw_sem.at[side, i]),
                    sraw.at[side, i],
                    suf.at[side, i],
                )
            )
        raw.append(
            (
                pltpu.make_async_copy(prefix_hbm.at[side], praw.at[side], raw_sem.at[side, OWN]),
                praw.at[side],
                pre.at[side],
            )
        )
    for copy, _, _ in raw:
        copy.start()
    load_wo.start()

    wide = 256
    for n in range(COLS // wide):
        cols = pl.ds(n * wide, wide)
        partial[:, cols] = jnp.dot(hidden[...], wq[:, cols], preferred_element_type=F32)
    values = hidden[...].astype(F32)
    values = values * values
    partial[:, COLS:] = split_lanes(values[:, :128] + values[:, 128:])

    pl.semaphore_wait(barrier, NZ - 1 + NY - 1 + NP - 1)

    for k in range(1, NY):
        first = pl.multiple_of(lax.rem(y + k, NY) * NZ * OWN, NZ * OWN)
        block = partial[pl.ds(first, NZ * OWN), :].astype(BF16)
        for j in range(NZ):
            ysend[k - 1, j] = block[OWN * j : OWN * (j + 1)]
    ycopies = []
    for n in FAR_FIRST:
        slot = lax.rem(z + n, NZ)
        for k in (2, 1, 3):
            copy = remote(
                ysend.at[k - 1, slot], yrecv.at[k - 1, n], ys.at[k - 1, n], yr.at[k - 1, n], at_y(k)
            )
            ycopies.append(start(copy))
    first = pl.multiple_of(y * NZ * OWN, NZ * OWN)
    block = partial[pl.ds(first, NZ * OWN), :]
    for j in range(NZ):
        mine[j] = block[OWN * j : OWN * (j + 1)]

    for copy, source, target in raw[: OWN + 1]:
        copy.wait()
        regroup(source, target)
    zcopies = []
    for m, n in enumerate(FAR_FIRST):
        slot = lax.rem(z + n, NZ)
        summed = mine[slot]
        for i, k in enumerate((2, 1, 3)):
            ycopies[(NY - 1) * m + i].wait_recv()
            summed = summed + yrecv[k - 1, n].astype(F32)
        if n == 0:
            mine[slot] = summed
            break
        zsend[n - 1, :, :COLS] = summed[:, :COLS].astype(BF16)
        zsend[n - 1, :, COLS:] = split_lanes(summed[:, COLS:]).astype(BF16)
        copy = remote(zsend.at[n - 1], zrecv.at[n - 1], zs.at[n - 1], zr.at[n - 1], at_z(n))
        zcopies.append(start(copy))
    for copy, source, target in raw[OWN + 1 :]:
        copy.wait()
        regroup(source, target)
    for copy in zcopies:
        copy.wait_recv()
    own = mine[z]
    for k in range(1, NZ):
        own = own + zrecv[k - 1].astype(F32)
    mean_sq = jnp.sum(own[:, COLS:], axis=1, keepdims=True) * (1.0 / D)
    scaled = own[:, :COLS] * lax.rsqrt(mean_sq + EPSILON)
    for r in range(REP):
        qrows[OWN * r : OWN * (r + 1), :] = scaled[:, HD * r : HD * (r + 1)]
    qall[p] = jnp.concatenate(
        [qrows[pl.ds(i, REP, stride=OWN), :] for i in range(OWN)], axis=0
    ).astype(BF16)
    for k, (dx, dc) in enumerate(others[::-1]):
        copy = remote(qall.at[p], qall.at[p], qs.at[k], qr.at[p], (prefix_of(dx, dc), s))
        start(copy)

    first_position = p * SPAN
    place = lax.broadcasted_iota(jnp.int32, (REP, SPAN), 1) + first_position
    live = [place < lengths[i] for i in range(OWN)]
    row_id = lax.broadcasted_iota(jnp.int32, (ROWS, 128), 0)
    lane_id = lax.broadcasted_iota(jnp.int32, (ROWS, 128), 1)
    diagonal = row_id == lane_id
    top_row = lax.broadcasted_iota(jnp.int32, (8, 128), 0) == 0

    def attend(g):
        q = qall[g]
        raw_scores = across(q, pre[0, g])
        prefix_scores = jnp.concatenate(
            [
                raw_scores[:, BLOCK * b : BLOCK * (b + 1)] * (scale[0, b, g] * SCALING)
                for b in range(SPAN // BLOCK)
            ],
            axis=1,
        )
        pieces = []
        for i in range(OWN):
            pair = q[16 * (i // 2) : 16 * (i // 2 + 1)]
            score = across(pair, suf[0, i, g])[8 * (i % 2) : 8 * (i % 2) + 8] * SCALING
            pieces.append(jnp.where(live[i], score, -jnp.inf))
        suffix_scores = jnp.concatenate(pieces, axis=0)
        peak = jnp.maximum(
            jnp.max(prefix_scores, axis=1, keepdims=True), jnp.max(suffix_scores, axis=1, keepdims=True)
        )
        prefix_exp = jnp.exp(prefix_scores - peak)
        suffix_exp = jnp.exp(suffix_scores - peak)
        total = jnp.sum(prefix_exp, axis=1, keepdims=True) + jnp.sum(suffix_exp, axis=1, keepdims=True)
        prefix_weights = jnp.concatenate(
            [
                prefix_exp[:, BLOCK * b : BLOCK * (b + 1)] * scale[1, b, g]
                for b in range(SPAN // BLOCK)
            ],
            axis=1,
        ).astype(BF16)
        suffix_weights = suffix_exp.astype(BF16)
        weighted = jnp.dot(prefix_weights, pre[1, g], preferred_element_type=F32)
        pieces = []
        for i in range(OWN):
            pair = suffix_weights[16 * (i // 2) : 16 * (i // 2 + 1)]
            value = jnp.dot(pair, suf[1, i, g], preferred_element_type=F32)
            pieces.append(value[8 * (i % 2) : 8 * (i % 2) + 8])
        csend[g, :ROWS] = weighted + jnp.concatenate(pieces, axis=0)
        peak_row = jnp.sum(jnp.where(diagonal, peak, 0.0), axis=0, keepdims=True)
        total_row = jnp.sum(jnp.where(diagonal, total, 0.0), axis=0, keepdims=True)
        csend[g, ROWS:] = jnp.where(top_row, peak_row, total_row)

    for dx in X_ORDER:
        for dc in range(NC):
            if dx or dc:
                g = prefix_of(dx, dc)
                remote(qall.at[g], qall.at[g], qs.at[0], qr.at[g], (g, s)).wait_recv()
        for dc in range(NC):
            attend(prefix_of(dx, dc))
        for dc in range(NC):
            if dx or dc:
                g = prefix_of(dx, dc)
                start(remote(csend.at[g], crecv.at[p], cs.at[g], cr.at[p], (g, s)))

    for dx, dc in others:
        g = prefix_of(dx, dc)
        remote(csend.at[g], crecv.at[g], cs.at[g], cr.at[g], (g, s)).wait_recv()

    parts = [csend[p]] + [crecv[prefix_of(dx, dc)] for dx, dc in others]
    peaks = [part[ROWS : ROWS + 1] for part in parts]
    totals = [part[ROWS + 1 : ROWS + 2] for part in parts]
    top = functools.reduce(jnp.maximum, peaks)
    factors = [jnp.exp(peak - top) for peak in peaks]
    whole = functools.reduce(jnp.add, [f * t for f, t in zip(factors, totals)])
    attended = None
    for part, factor in zip(parts, factors):
        share = jnp.sum(jnp.where(diagonal, factor / whole, 0.0), axis=1, keepdims=True)
        term = part[:ROWS] * share
        attended = term if attended is None else attended + term
    heads[y, z] = attended.astype(BF16)
    for k in FAR_FIRST[:-1]:
        start(remote(heads.at[y, z], heads.at[y, z], gs.at[k - 1], gr.at[z], at_z(k)))
    load_wo.wait()
    for n in NEAR_FIRST:
        slot = lax.rem(z + n, NZ)
        if n:
            remote(heads.at[y, slot], heads.at[y, slot], gs.at[n - 1], gr.at[slot], at_z(n)).wait_recv()
        for k in (2, 1, 3):
            start(
                remote(
                    heads.at[y, slot], heads.at[y, slot], hs.at[k - 1, slot], hr.at[y, slot], at_y(k)
                )
            )
    for k in (0, 1, 3, 2):
        block = lax.rem(y + k, NY)
        if k:
            for j in range(NZ):
                remote(
                    heads.at[block, j], heads.at[block, j], hs.at[k - 1, j], hr.at[block, j], at_y(k)
                ).wait_recv()
        rows = jnp.swapaxes(heads[block].reshape(NZ * OWN, REP, HD), 0, 1)
        rows = jnp.concatenate([rows[r] for r in range(REP)], axis=1)
        product = jnp.dot(rows, wo[...], preferred_element_type=F32).astype(BF16)
        for half in range(2):
            g = block * 2 + half
            osend[g] = product[16 * half : 16 * (half + 1)]

            @pl.when(g != p)
            def _():
                remote(osend.at[g], orecv.at[p], os_.at[g], or_.at[p], (g, s)).start()

    for dx, dc in others:
        g = prefix_of(dx, dc)
        remote(osend.at[g], orecv.at[g], os_.at[g], or_.at[g], (g, s)).wait_recv()
    result = osend[p].astype(F32)
    for dx, dc in others:
        result = result + orecv[prefix_of(dx, dc)].astype(F32)
    out[...] = result.astype(BF16)

    for copy in pending:
        copy.wait_send()
    for dx, dc in others:
        g = prefix_of(dx, dc)
        remote(osend.at[g], orecv.at[p], os_.at[g], or_.at[p], (g, s)).wait_send()


def on_device(
    hidden_states, query_weight, prefix_levels, prefix_scale, suffix_cache, lengths, output_weight
):
    anywhere = pl.BlockSpec(memory_space=pl.ANY)
    scalar = pl.BlockSpec(memory_space=pltpu.SMEM)
    dma = pltpu.SemaphoreType.DMA
    call = pl.pallas_call(
        kernel,
        out_shape=jax.ShapeDtypeStruct((16, 256), BF16),
        in_specs=[scalar, scalar] + [anywhere] * 5,
        out_specs=pl.BlockSpec(memory_space=pltpu.VMEM),
        scratch_shapes=[
            pltpu.VMEM((128, 256), BF16),
            pltpu.VMEM((256, COLS), BF16),
            pltpu.VMEM((COLS, 256), BF16),
            pltpu.VMEM((2, SPAN * GROUPS, HD), BF16),
            pltpu.VMEM((2, OWN, SPAN * GROUPS, HD), BF16),
            pltpu.VMEM((2, GROUPS, SPAN, HD), BF16),
            pltpu.VMEM((2, OWN, GROUPS, SPAN, HD), BF16),
            pltpu.VMEM((128, WIDE), F32),
            pltpu.VMEM((NY - 1, NZ, OWN, WIDE), BF16),
            pltpu.VMEM((NY - 1, NZ, OWN, WIDE), BF16),
            pltpu.VMEM((NZ, OWN, WIDE), F32),
            pltpu.VMEM((NZ - 1, OWN, WIDE), BF16),
            pltpu.VMEM((NZ - 1, OWN, WIDE), BF16),
            pltpu.VMEM((ROWS, HD), F32),
            pltpu.VMEM((NP, ROWS, HD), BF16),
            pltpu.VMEM((NP, ROWS + 8, HD), F32),
            pltpu.VMEM((NP, ROWS + 8, HD), F32),
            pltpu.VMEM((NY, NZ, ROWS, HD), BF16),
            pltpu.VMEM((NP, 16, 256), BF16),
            pltpu.VMEM((NP, 16, 256), BF16),
            dma((3,)),
            dma((2, OWN + 1)),
            dma((NY - 1, NZ)),
            dma((NY - 1, NZ)),
            dma((NZ - 1,)),
            dma((NZ - 1,)),
            dma((NP - 1,)),
            dma((NP,)),
            dma((NP,)),
            dma((NP,)),
            dma((NZ - 1,)),
            dma((NZ,)),
            dma((NY - 1, NZ)),
            dma((NY, NZ)),
            dma((NP,)),
            dma((NP,)),
        ],
        compiler_params=pltpu.CompilerParams(
            collective_id=0, has_side_effects=True, vmem_limit_bytes=60 * 2**20
        ),
        name="layer",
    )
    return call(
        prefix_scale,
        lengths,
        hidden_states,
        query_weight,
        prefix_levels.reshape(2, SPAN * GROUPS, HD),
        suffix_cache.reshape(2, OWN, SPAN * GROUPS, HD),
        output_weight,
    )


def solution(mesh):
    return jax.shard_map(
        on_device,
        mesh=mesh,
        in_specs=(
            P(None, "sample"),
            P("sample", "prefix"),
            P(None, "prefix", None, None),
            P(None, "prefix", None),
            P(None, "sample", "prefix", None, None),
            P("sample"),
            P("prefix", "sample"),
        ),
        out_specs=P("prefix", "sample"),
        check_vma=False,
    )
```

time: 97.7 us -> 43.6 us (0.45)
  the two profiles are of different devices: /device:TPU:1 before, /device:TPU:5 now
where the time goes in v1:
time: 43.6 us; the launch traced here: 43.4 us
  Pallas kernels  42.1 us (97%)
  local copies, waits for them, and re-layouts  1.3 us (3%)
    pallas_call x1, Pallas kernels, on_device(): call(prefix_scale, lengths, hidden_states, query_weight, prefix_levels.re...  42.1 us
    unnamed x1, local copies, waits for them, and re-layouts  1.3 us

profile of v1, /device:TPU:5, one launch (start us, length us, event | category | flops | bytes accessed | tf_op | source)
XLA Modules:
  0.0 43.4 jit_solution(3655176046519817185)
XLA Ops:
  0.0 42.1 %layer.1 = bf16[16,256]{1,0:T(8,128)(2,1)} custom-call(f32[2,4,8]{2,1,0:T(4,128)} %scale.1, s32[4]{0:T(128)} %lengths.1, bf16[128,256]{1,0:T(8,128)(2,1)} %hidden_hbm.1, bf16[256,1024]{1,0:T(8,128)(2,1)} %wq_hbm.1, bf16[2,4096,128]{2,1,0:T(8,128)(2,1)} %bitcast.3, bf16[2,4,4096,128]{3,2,1,0:T(8,128)(2,1)} %bitcast.2, bf16[1024,256]{1,0:T(8,128)(2,1)} %wo_hbm.1), custom_call_target="tpu_custom_call" | custom-call | tf_op jit(solution)/shard_map/layer/pallas_call | solution.py:367
  42.1 1.3 %copy.9 = bf16[16,256]{1,0:T(8,128)(2,1)} copy(bf16[16,256]{1,0:T(8,128)(2,1)} %layer.1) | data formatting | bytes 16384

commit v2 on v1

--- a/solution.py
+++ b/solution.py
@@ -52,10 +52,10 @@
 
 
 def kernel(
-    scale, lengths, hidden_hbm, wq_hbm, prefix_hbm, suffix_hbm, wo_hbm, out,
+    scale_hbm, lengths_hbm, hidden_hbm, wq_hbm, prefix_hbm, suffix_hbm, wo_hbm, out,
     hidden, wq, wo, praw, sraw, pre, suf, partial, ysend, yrecv, mine, zsend, zrecv, qrows, qall,
     csend, crecv, heads, osend, orecv,
-    load_sem, raw_sem, ys, yr, zs, zr, qs, qr, cs, cr, gs, gr, hs, hr, os_, or_,
+    scale, lengths, ready, load_sem, raw_sem, ys, yr, zs, zr, qs, qr, cs, cr, gs, gr, hs, hr, os_, or_,
 ):
     p = lax.axis_index("prefix")
     s = lax.axis_index("sample")
@@ -88,11 +88,15 @@
     load_hidden = pltpu.make_async_copy(hidden_hbm, hidden, load_sem.at[0])
     load_wq = pltpu.make_async_copy(wq_hbm, wq, load_sem.at[1])
     load_wo = pltpu.make_async_copy(wo_hbm, wo, load_sem.at[2])
+    load_scale = pltpu.make_async_copy(scale_hbm, scale, load_sem.at[3])
+    load_lengths = pltpu.make_async_copy(lengths_hbm, lengths, load_sem.at[4])
     load_hidden.start()
     load_wq.start()
+    load_scale.start()
+    load_lengths.start()
 
     barrier = pltpu.get_barrier_semaphore()
-    for k in range(1, NZ):
+    for k in (1, NZ - 1):
         pl.semaphore_signal(barrier, inc=1, device_id=at_z(k), device_id_type=MESH)
     for k in range(1, NY):
         pl.semaphore_signal(barrier, inc=1, device_id=at_y(k), device_id_type=MESH)
@@ -131,7 +135,9 @@
     values = values * values
     partial[:, COLS:] = split_lanes(values[:, :128] + values[:, 128:])
 
-    pl.semaphore_wait(barrier, NZ - 1 + NY - 1 + NP - 1)
+    pl.semaphore_wait(barrier, 2 + NY - 1 + NP - 1)
+    for k in (1, NZ - 1):
+        pl.semaphore_signal(ready.at[0], inc=1, device_id=at_z(k), device_id_type=MESH)
 
     for k in range(1, NY):
         first = pl.multiple_of(lax.rem(y + k, NY) * NZ * OWN, NZ * OWN)
@@ -151,9 +157,14 @@
     for j in range(NZ):
         mine[j] = block[OWN * j : OWN * (j + 1)]
 
-    for copy, source, target in raw[: OWN + 1]:
+    for n, (copy, source, target) in enumerate(raw[: OWN + 1]):
         copy.wait()
         regroup(source, target)
+        if n == 1:
+            pl.semaphore_wait(ready.at[0], 2)
+            for k in (2, NZ - 2):
+                pl.semaphore_signal(ready.at[1], inc=1, device_id=at_z(k), device_id_type=MESH)
+    pl.semaphore_wait(ready.at[1], 2)
     zcopies = []
     for m, n in enumerate(FAR_FIRST):
         slot = lax.rem(z + n, NZ)
@@ -187,6 +198,8 @@
         copy = remote(qall.at[p], qall.at[p], qs.at[k], qr.at[p], (prefix_of(dx, dc), s))
         start(copy)
 
+    load_scale.wait()
+    load_lengths.wait()
     first_position = p * SPAN
     place = lax.broadcasted_iota(jnp.int32, (REP, SPAN), 1) + first_position
     live = [place < lengths[i] for i in range(OWN)]
@@ -318,8 +331,8 @@
     dma = pltpu.SemaphoreType.DMA
     call = pl.pallas_call(
         kernel,
-        out_shape=jax.ShapeDtypeStruct((16, 256), BF16),
-        in_specs=[scalar, scalar] + [anywhere] * 5,
+        out_shape=pltpu.VMEM((16, 256), BF16),
+        in_specs=[anywhere] * 7,
         out_specs=pl.BlockSpec(memory_space=pltpu.VMEM),
         scratch_shapes=[
             pltpu.VMEM((128, 256), BF16),
@@ -342,7 +355,10 @@
             pltpu.VMEM((NY, NZ, ROWS, HD), BF16),
             pltpu.VMEM((NP, 16, 256), BF16),
             pltpu.VMEM((NP, 16, 256), BF16),
-            dma((3,)),
+            pltpu.SMEM((2, 4, 8), F32),
+            pltpu.SMEM((4,), jnp.int32),
+            pltpu.SemaphoreType.REGULAR((2,)),
+            dma((5,)),
             dma((2, OWN + 1)),
             dma((NY - 1, NZ)),
             dma((NY - 1, NZ)),

time: 43.6 us -> 40.5 us (0.929)
  Pallas kernels: 42.1 us -> 39.8 us
  local copies, waits for them, and re-layouts: 1.3 us -> 0.6 us
    pallas_call x1, Pallas kernels: 42.1 us -> 39.8 us  [on_device(): call(prefix_scale, lengths, hidden_states, query_weight, prefix_levels.re...]
    unnamed x1, local copies, waits for them, and re-layouts: 1.3 us -> 0.6 us
where the time goes in v2:
time: 40.5 us; the launch traced here: 40.4 us
  Pallas kernels  39.8 us (98%)
  local copies, waits for them, and re-layouts  0.6 us (1%)
    pallas_call x1, Pallas kernels, on_device(): call(prefix_scale, lengths, hidden_states, query_weight, prefix_levels.re...  39.8 us

profile of v2, /device:TPU:5, one launch (start us, length us, event | category | flops | bytes accessed | tf_op | source)
XLA Modules:
  0.0 40.4 jit_solution(13876792533689438255)
XLA Ops:
  0.0 39.8 %layer.1 = bf16[16,256]{1,0:T(8,128)(2,1)S(1)} custom-call(f32[2,4,8]{2,1,0:T(4,128)} %scale_hbm.1, s32[4]{0:T(128)} %lengths_hbm.1, bf16[128,256]{1,0:T(8,128)(2,1)} %hidden_hbm.1, bf16[256,1024]{1,0:T(8,128)(2,1)} %wq_hbm.1, bf16[2,4096,128]{2,1,0:T(8,128)(2,1)} %bitcast.3, bf16[2,4,4096,128]{3,2,1,0:T(8,128)(2,1)} %bitcast.2, bf16[1024,256]{1,0:T(8,128)(2,1)} %wo_hbm.1), custom_call_target="tpu_custom_call" | custom-call | tf_op jit(solution)/shard_map/layer/pallas_call | solution.py:383
  39.8 0.6 %copy.9 = bf16[16,256]{1,0:T(8,128)(2,1)} copy(bf16[16,256]{1,0:T(8,128)(2,1)S(1)} %layer.1) | data formatting | bytes 16384

commit v3 on v2

--- a/solution.py
+++ b/solution.py
@@ -24,6 +24,8 @@
 D = 8192
 SCALING = 1.0 / math.sqrt(HD)
 X_ORDER = (0, 1, 3, 2)
+TURNS = (((0, 0), (0, 1)), ((1, 0), (1, 1), (3, 0), (3, 1)), ((2, 0), (2, 1)))
+PAIRS = (2, 1, 3, 0)
 FAR_FIRST = (4, 3, 5, 2, 6, 1, 7, 0)
 NEAR_FIRST = FAR_FIRST[::-1]
 F32 = jnp.float32
@@ -53,7 +55,7 @@
 
 def kernel(
     scale_hbm, lengths_hbm, hidden_hbm, wq_hbm, prefix_hbm, suffix_hbm, wo_hbm, out,
-    hidden, wq, wo, praw, sraw, pre, suf, partial, ysend, yrecv, mine, zsend, zrecv, qrows, qall,
+    hidden, wq, wo, praw, sraw, pre, suf, partial, ysend, yrecv, mine, kept, zsend, zrecv, qrows, qall,
     csend, crecv, heads, osend, orecv,
     scale, lengths, ready, load_sem, raw_sem, ys, yr, zs, zr, qs, qr, cs, cr, gs, gr, hs, hr, os_, or_,
 ):
@@ -113,7 +115,7 @@
                 (
                     pltpu.make_async_copy(suffix_hbm.at[side, i], sraw.at[side, i], raw_sem.at[side, i]),
                     sraw.at[side, i],
-                    suf.at[side, i],
+                    suf.at[side, i // 2, :, :, pl.ds(HD * (i % 2), HD)],
                 )
             )
         raw.append(
@@ -139,23 +141,24 @@
     for k in (1, NZ - 1):
         pl.semaphore_signal(ready.at[0], inc=1, device_id=at_z(k), device_id_type=MESH)
 
+    pairs, tall = NZ // 2, 2 * OWN
     for k in range(1, NY):
         first = pl.multiple_of(lax.rem(y + k, NY) * NZ * OWN, NZ * OWN)
         block = partial[pl.ds(first, NZ * OWN), :].astype(BF16)
-        for j in range(NZ):
-            ysend[k - 1, j] = block[OWN * j : OWN * (j + 1)]
+        for j in range(pairs):
+            ysend[k - 1, j] = block[tall * j : tall * (j + 1)]
     ycopies = []
-    for n in FAR_FIRST:
-        slot = lax.rem(z + n, NZ)
+    for m in PAIRS:
+        slot = lax.rem(z // 2 + m, pairs)
         for k in (2, 1, 3):
             copy = remote(
-                ysend.at[k - 1, slot], yrecv.at[k - 1, n], ys.at[k - 1, n], yr.at[k - 1, n], at_y(k)
+                ysend.at[k - 1, slot], yrecv.at[k - 1, m], ys.at[k - 1, m], yr.at[k - 1, m], at_y(k)
             )
             ycopies.append(start(copy))
     first = pl.multiple_of(y * NZ * OWN, NZ * OWN)
     block = partial[pl.ds(first, NZ * OWN), :]
-    for j in range(NZ):
-        mine[j] = block[OWN * j : OWN * (j + 1)]
+    for j in range(pairs):
+        mine[j] = block[tall * j : tall * (j + 1)]
 
     for n, (copy, source, target) in enumerate(raw[: OWN + 1]):
         copy.wait()
@@ -165,28 +168,35 @@
             for k in (2, NZ - 2):
                 pl.semaphore_signal(ready.at[1], inc=1, device_id=at_z(k), device_id_type=MESH)
     pl.semaphore_wait(ready.at[1], 2)
-    zcopies = []
-    for m, n in enumerate(FAR_FIRST):
-        slot = lax.rem(z + n, NZ)
+    for i, m in enumerate(PAIRS):
+        slot = lax.rem(z // 2 + m, pairs)
         summed = mine[slot]
-        for i, k in enumerate((2, 1, 3)):
-            ycopies[(NY - 1) * m + i].wait_recv()
-            summed = summed + yrecv[k - 1, n].astype(F32)
-        if n == 0:
-            mine[slot] = summed
-            break
-        zsend[n - 1, :, :COLS] = summed[:, :COLS].astype(BF16)
-        zsend[n - 1, :, COLS:] = split_lanes(summed[:, COLS:]).astype(BF16)
-        copy = remote(zsend.at[n - 1], zrecv.at[n - 1], zs.at[n - 1], zr.at[n - 1], at_z(n))
-        zcopies.append(start(copy))
+        for j, k in enumerate((2, 1, 3)):
+            ycopies[(NY - 1) * i + j].wait_recv()
+            summed = summed + yrecv[k - 1, m].astype(F32)
+        squares = split_lanes(summed[:, COLS:])
+        for half in range(2):
+            rows = slice(OWN * half, OWN * (half + 1))
+            target = slot * 2 + half
+            zsend[target, :, :COLS] = summed[rows, :COLS].astype(BF16)
+            zsend[target, :, COLS:] = squares[rows].astype(BF16)
+            if m:
+                start(
+                    remote(zsend.at[target], zrecv.at[z], zs.at[target], zr.at[z], (p, y * NZ + target))
+                )
+            else:
+                kept[half] = summed[rows]
+    beside = z + 1 - 2 * (z % 2)
+    start(remote(zsend.at[beside], zrecv.at[z], zs.at[beside], zr.at[z], (p, y * NZ + beside)))
     for copy, source, target in raw[OWN + 1 :]:
         copy.wait()
         regroup(source, target)
-    for copy in zcopies:
-        copy.wait_recv()
-    own = mine[z]
     for k in range(1, NZ):
-        own = own + zrecv[k - 1].astype(F32)
+        slot = lax.rem(z + k, NZ)
+        remote(zsend.at[slot], zrecv.at[slot], zs.at[slot], zr.at[slot], at_z(k)).wait_recv()
+    own = kept[z % 2]
+    for k in range(1, NZ):
+        own = own + zrecv[lax.rem(z + k, NZ)].astype(F32)
     mean_sq = jnp.sum(own[:, COLS:], axis=1, keepdims=True) * (1.0 / D)
     scaled = own[:, :COLS] * lax.rsqrt(mean_sq + EPSILON)
     for r in range(REP):
@@ -202,7 +212,8 @@
     load_lengths.wait()
     first_position = p * SPAN
     place = lax.broadcasted_iota(jnp.int32, (REP, SPAN), 1) + first_position
-    live = [place < lengths[i] for i in range(OWN)]
+    live = jnp.concatenate([place < lengths[i] for i in range(OWN)], axis=0)
+    upper = lax.broadcasted_iota(jnp.int32, (16, HD), 0) < REP
     row_id = lax.broadcasted_iota(jnp.int32, (ROWS, 128), 0)
     lane_id = lax.broadcasted_iota(jnp.int32, (ROWS, 128), 1)
     diagonal = row_id == lane_id
@@ -219,11 +230,11 @@
             axis=1,
         )
         pieces = []
-        for i in range(OWN):
-            pair = q[16 * (i // 2) : 16 * (i // 2 + 1)]
-            score = across(pair, suf[0, i, g])[8 * (i % 2) : 8 * (i % 2) + 8] * SCALING
-            pieces.append(jnp.where(live[i], score, -jnp.inf))
-        suffix_scores = jnp.concatenate(pieces, axis=0)
+        for j in range(OWN // 2):
+            pair = q[16 * j : 16 * (j + 1)]
+            both = jnp.concatenate([jnp.where(upper, pair, 0), jnp.where(upper, 0, pair)], axis=1)
+            pieces.append(across(both, suf[0, j, g]))
+        suffix_scores = jnp.where(live, jnp.concatenate(pieces, axis=0) * SCALING, -jnp.inf)
         peak = jnp.maximum(
             jnp.max(prefix_scores, axis=1, keepdims=True), jnp.max(suffix_scores, axis=1, keepdims=True)
         )
@@ -240,23 +251,23 @@
         suffix_weights = suffix_exp.astype(BF16)
         weighted = jnp.dot(prefix_weights, pre[1, g], preferred_element_type=F32)
         pieces = []
-        for i in range(OWN):
-            pair = suffix_weights[16 * (i // 2) : 16 * (i // 2 + 1)]
-            value = jnp.dot(pair, suf[1, i, g], preferred_element_type=F32)
-            pieces.append(value[8 * (i % 2) : 8 * (i % 2) + 8])
+        for j in range(OWN // 2):
+            pair = suffix_weights[16 * j : 16 * (j + 1)]
+            value = jnp.dot(pair, suf[1, j, g], preferred_element_type=F32)
+            pieces += [value[:REP, :HD], value[REP:, HD:]]
         csend[g, :ROWS] = weighted + jnp.concatenate(pieces, axis=0)
         peak_row = jnp.sum(jnp.where(diagonal, peak, 0.0), axis=0, keepdims=True)
         total_row = jnp.sum(jnp.where(diagonal, total, 0.0), axis=0, keepdims=True)
         csend[g, ROWS:] = jnp.where(top_row, peak_row, total_row)
 
-    for dx in X_ORDER:
-        for dc in range(NC):
+    for together in TURNS:
+        for dx, dc in together:
             if dx or dc:
                 g = prefix_of(dx, dc)
                 remote(qall.at[g], qall.at[g], qs.at[0], qr.at[g], (g, s)).wait_recv()
-        for dc in range(NC):
+        for dx, dc in together:
             attend(prefix_of(dx, dc))
-        for dc in range(NC):
+        for dx, dc in together:
             if dx or dc:
                 g = prefix_of(dx, dc)
                 start(remote(csend.at[g], crecv.at[p], cs.at[g], cr.at[p], (g, s)))
@@ -341,13 +352,14 @@
             pltpu.VMEM((2, SPAN * GROUPS, HD), BF16),
             pltpu.VMEM((2, OWN, SPAN * GROUPS, HD), BF16),
             pltpu.VMEM((2, GROUPS, SPAN, HD), BF16),
-            pltpu.VMEM((2, OWN, GROUPS, SPAN, HD), BF16),
+            pltpu.VMEM((2, OWN // 2, GROUPS, SPAN, 2 * HD), BF16),
             pltpu.VMEM((128, WIDE), F32),
-            pltpu.VMEM((NY - 1, NZ, OWN, WIDE), BF16),
-            pltpu.VMEM((NY - 1, NZ, OWN, WIDE), BF16),
-            pltpu.VMEM((NZ, OWN, WIDE), F32),
-            pltpu.VMEM((NZ - 1, OWN, WIDE), BF16),
-            pltpu.VMEM((NZ - 1, OWN, WIDE), BF16),
+            pltpu.VMEM((NY - 1, NZ // 2, 2 * OWN, WIDE), BF16),
+            pltpu.VMEM((NY - 1, NZ // 2, 2 * OWN, WIDE), BF16),
+            pltpu.VMEM((NZ // 2, 2 * OWN, WIDE), F32),
+            pltpu.VMEM((2, OWN, WIDE), F32),
+            pltpu.VMEM((NZ, OWN, WIDE), BF16),
+            pltpu.VMEM((NZ, OWN, WIDE), BF16),
             pltpu.VMEM((ROWS, HD), F32),
             pltpu.VMEM((NP, ROWS, HD), BF16),
             pltpu.VMEM((NP, ROWS + 8, HD), F32),
@@ -360,10 +372,10 @@
             pltpu.SemaphoreType.REGULAR((2,)),
             dma((5,)),
             dma((2, OWN + 1)),
-            dma((NY - 1, NZ)),
-            dma((NY - 1, NZ)),
-            dma((NZ - 1,)),
-            dma((NZ - 1,)),
+            dma((NY - 1, NZ // 2)),
+            dma((NY - 1, NZ // 2)),
+            dma((NZ,)),
+            dma((NZ,)),
             dma((NP - 1,)),
             dma((NP,)),
             dma((NP,)),

time: 40.5 us -> 40.4 us (level)
    pallas_call x1, Pallas kernels: 39.8 us -> 39.4 us  [on_device(): call(prefix_scale, lengths, hidden_states, query_weight, prefix_levels.re...]
where the time goes in v3:
time: 40.4 us; the launch traced here: 40 us
  Pallas kernels  39.4 us (98%)
  local copies, waits for them, and re-layouts  0.6 us (1%)
    pallas_call x1, Pallas kernels, on_device(): call(prefix_scale, lengths, hidden_states, query_weight, prefix_levels.re...  39.4 us

profile of v3, /device:TPU:5, one launch (start us, length us, event | category | flops | bytes accessed | tf_op | source)
XLA Modules:
  0.0 40.0 jit_solution(7565326780227638969)
XLA Ops:
  0.0 39.4 %layer.1 = bf16[16,256]{1,0:T(8,128)(2,1)S(1)} custom-call(f32[2,4,8]{2,1,0:T(4,128)} %scale_hbm.1, s32[4]{0:T(128)} %lengths_hbm.1, bf16[128,256]{1,0:T(8,128)(2,1)} %hidden_hbm.1, bf16[256,1024]{1,0:T(8,128)(2,1)} %wq_hbm.1, bf16[2,4096,128]{2,1,0:T(8,128)(2,1)} %bitcast.3, bf16[2,4,4096,128]{3,2,1,0:T(8,128)(2,1)} %bitcast.2, bf16[1024,256]{1,0:T(8,128)(2,1)} %wo_hbm.1), custom_call_target="tpu_custom_call" | custom-call | tf_op jit(solution)/shard_map/layer/pallas_call | solution.py:395
  39.4 0.6 %copy.9 = bf16[16,256]{1,0:T(8,128)(2,1)} copy(bf16[16,256]{1,0:T(8,128)(2,1)S(1)} %layer.1) | data formatting | bytes 16384
